TPU v7x, 512 devices: a whole 4x4x16 slice. The times are simulated.
512 devices in a mesh: mem: 8 (over y, z_hi), gx: 64 (over x, z_lo, core).
Axes of the slice: x: 4, y: 4, z: 16 (z_hi: 2, z_lo: 8; z = z_hi * 8 + z_lo), core: 2. Of those that a mesh axis runs over, the one named last changes fastest.
Arguments:
- density: float32 [128, 512, 256], P('mem', 'gx'), may hold values from 0.5 to 2
- momenta: float32 [128, 2, 512, 256], P('mem', None, 'gx'), may hold values from -1 to 1
- desired: float32 [2, 512, 256], P(None, 'gx'), may hold values from -1.5 to 1.5
- factor_x: float32 [512, 128], P('gx'), may hold values from -1 to 1, as said below
- factor_y: float32 [256, 128], replicated, may hold values from -1 to 1, as said below
- factor_m: float32 [128, 32], P('mem'), may hold values from -1 to 1, as said below
Outputs:
- core: float32 [32, 3, 128, 128], P('mem', None, 'gx')
Inputs may be any that keep to these rules, and one draw needn't show every extreme that they name: `factor_x`: columns are orthonormal. `factor_y`: columns are orthonormal. `factor_m`: columns are orthonormal.
All inputs are finite; a program needn't handle non-finite values.
Results may differ from a plain program's by a relative error of at most 0.00013.
Values sent between devices are 32-bit elements; how exact they have to be, the bound alone decides.
A program may use at most 64 MiB of HBM per device.

v0:
```python
import jax
import jax.numpy as jnp
from jax import lax
from jax.sharding import PartitionSpec as P

STEPS = 2


STIFF = 1.0
RELAX = 1.0
DTIME = 0.2


def with_halo(cells, sides, width):
    for axis, dim in sides:
        count = lax.axis_size(axis)
        head = lax.slice_in_dim(cells, 0, width, axis=dim)
        tail = lax.slice_in_dim(cells, cells.shape[dim] - width, cells.shape[dim], axis=dim)
        cells = jnp.concatenate(
            [
                lax.ppermute(tail, axis, [(i, (i + 1) % count) for i in range(count)]),
                cells,
                lax.ppermute(head, axis, [((i + 1) % count, i) for i in range(count)]),
            ],
            axis=dim,
        )
    return cells


def tendency(fields, desired):
    density = fields[:, 0]
    moment_x = fields[:, 1]
    moment_y = fields[:, 2]
    speed_x = moment_x / density
    speed_y = moment_y / density
    sound = jnp.sqrt(STIFF * density)
    pressure = 0.5 * STIFF * density * density
    conserved = (density, moment_x, moment_y)
    fluxes_x = (moment_x, moment_x * speed_x + pressure, moment_y * speed_x)
    fluxes_y = (moment_y, moment_x * speed_y, moment_y * speed_y + pressure)
    reach_x = jnp.abs(speed_x) + sound
    bound_x = jnp.maximum(reach_x[:, :-1], reach_x[:, 1:])
    reach_y = (jnp.abs(speed_y) + sound)[:, 1:-1]
    bound_y = jnp.maximum(reach_y, jnp.roll(reach_y, -1, axis=-1))
    changes = []
    for quantity, normal_flux, cross_flux in zip(conserved, fluxes_x, fluxes_y):
        face_x = 0.5 * (normal_flux[:, :-1] + normal_flux[:, 1:]) - 0.5 * bound_x * (
            quantity[:, 1:] - quantity[:, :-1]
        )
        middle = quantity[:, 1:-1]
        cross_mid = cross_flux[:, 1:-1]
        face_y = 0.5 * (cross_mid + jnp.roll(cross_mid, -1, axis=-1)) - 0.5 * bound_y * (
            jnp.roll(middle, -1, axis=-1) - middle
        )
        changes.append(-(face_x[:, 1:] - face_x[:, :-1]) - (face_y - jnp.roll(face_y, 1, axis=-1)))
    centre = density[:, 1:-1]
    changes[1] = changes[1] + (centre * desired[0] - moment_x[:, 1:-1]) / RELAX
    changes[2] = changes[2] + (centre * desired[1] - moment_y[:, 1:-1]) / RELAX
    return jnp.stack(changes, axis=1)


def single_rims(fields):
    return with_halo(fields, (("gx", 2),), 1)


def on_device(density, momenta, desired, factor_x, factor_y, factor_m):
    highest = lax.Precision.HIGHEST
    fields = jnp.concatenate([density[:, None], momenta], axis=1)
    for repeat in range(STEPS):
        sectioned = fields + DTIME * tendency(single_rims(fields), desired)
        second = sectioned + DTIME * tendency(single_rims(sectioned), desired)
        fields = 0.5 * fields + 0.5 * second
    along_y = jnp.einsum("mcxy,yb->mcxb", fields, factor_y, precision=highest)
    along_x = jnp.einsum("mcxb,xa->mcab", along_y, factor_x, precision=highest)
    shared_x = lax.psum_scatter(along_x, "gx", scatter_dimension=2, tiled=True)
    member_terms = jnp.einsum("mcab,mk->kcab", shared_x, factor_m, precision=highest)
    core = lax.psum_scatter(member_terms, "mem", scatter_dimension=0, tiled=True)
    return core


def solution(mesh):
    return jax.shard_map(
        on_device,
        mesh=mesh,
        in_specs=(
            P("mem", "gx", None),
            P("mem", None, "gx", None),
            P(None, "gx", None),
            P("gx", None),
            P(),
            P("mem", None),
        ),
        out_specs=P("mem", None, "gx", None),
        check_vma=False,
    )
```

profile of v0, /device:TPU:6, one launch (start us, length us, event | category | flops | bytes accessed | tf_op | source)
XLA Modules:
  0.0 1097.5 jit_solution(3101001367603070410)
XLA Ops:
  6.5 1.2 fusion.152
  7.8 1.9 collective-permute-start
  9.7 12.9 %collective-permute-start.1 = (f32[16,3,1,256]{3,2,0,1:T(1,128)S(1)}, f32[16,3,1,256]{3,2,0,1:T(1,128)S(1)}, u32[]{:S(2)}, u32[]{:S(2)}) collective-permute-start(f32[16,3,1,256]{3,2,0,1:T(1,128)S(1)} %get-tuple-element.64), channel_id=1, source_target_pairs={{1,0},{2,1},{3,2},{4,3},{5,4},{6,5},{7,6},{8,7},{9,8},{10,9},{11,1... | collective-permute-start | bytes 147464 | tf_op jit(solution)/shard_map/ppermute | solution.py:23
  22.6 0.7 slice_bitcast_fusion.13
  23.3 1.0 collective-permute-done.1
  24.3 1.1 pad_maximum_fusion
  25.6 0.2 fusion.129
  27.1 0.3 fusion.39
  27.7 0.3 copy-done.1
  28.2 1.9 collective-permute-start.2
  30.1 11.4 %collective-permute-start.3 = (f32[16,3,1,256]{3,2,0,1:T(1,128)S(1)}, f32[16,3,1,256]{3,2,0,1:T(1,128)S(1)}, u32[]{:S(2)}, u32[]{:S(2)}) collective-permute-start(f32[16,3,1,256]{3,2,0,1:T(1,128)S(1)} %get-tuple-element.62), channel_id=1, source_target_pairs={{1,0},{2,1},{3,2},{4,3},{5,4},{6,5},{7,6},{8,7},{9,8},{10,9},{11,1... | collective-permute-start | bytes 147464 | tf_op jit(solution)/shard_map/ppermute | solution.py:23
  41.5 1.7 collective-permute-done.3
  45.0 0.3 fusion.31
  45.8 1.9 collective-permute-start.4
  47.7 11.2 %collective-permute-start.5 = (f32[16,3,1,256]{3,2,0,1:T(1,128)S(1)}, f32[16,3,1,256]{3,2,0,1:T(1,128)S(1)}, u32[]{:S(2)}, u32[]{:S(2)}) collective-permute-start(f32[16,3,1,256]{3,2,0,1:T(1,128)S(1)} %get-tuple-element.60), channel_id=1, source_target_pairs={{1,0},{2,1},{3,2},{4,3},{5,4},{6,5},{7,6},{8,7},{9,8},{10,9},{11,1... | collective-permute-start | bytes 147464 | tf_op jit(solution)/shard_map/ppermute | solution.py:23
  58.9 1.7 collective-permute-done.5
  60.7 0.2 fusion.137
  62.3 0.3 fusion.23
  63.0 1.9 collective-permute-start.6
  65.0 11.4 %collective-permute-start.7 = (f32[16,3,1,256]{3,2,0,1:T(1,128)S(1)}, f32[16,3,1,256]{3,2,0,1:T(1,128)S(1)}, u32[]{:S(2)}, u32[]{:S(2)}) collective-permute-start(f32[16,3,1,256]{3,2,0,1:T(1,128)S(1)} %get-tuple-element.58), channel_id=1, source_target_pairs={{1,0},{2,1},{3,2},{4,3},{5,4},{6,5},{7,6},{8,7},{9,8},{10,9},{11,1... | collective-permute-start | bytes 147464 | tf_op jit(solution)/shard_map/ppermute | solution.py:23
  76.3 1.5 collective-permute-done.7
  79.6 0.3 fusion.15
  80.3 0.6 fusion.6
  80.9 5.1 fusion.123
  86.0 2.4 copy.43
  88.5 1.3 dynamic-slice
  90.4 814.6 %all-reduce.5.cloned.1.call-done = f32[16,3,128,128]{3,0,2,1:T(8,128)} async-done(((f32[16,3,128,128]{3,0,2,1:T(8,128)}), f32[16,3,128,128]{3,0,2,1:T(8,128)}) %all-reduce.5.cloned.1.call-update) | async-done | bytes 3145744
  904.9 1.7 convolution_bitcast_fusion
  906.7 1.3 dynamic-slice.2
  908.6 180.7 %all-reduce.7.cloned.1.call-done = f32[32,3,2,128]{3,0,2,1:T(8,128)} async-done(((f32[32,3,2,128]{3,0,2,1:T(8,128)}), f32[32,3,2,128]{3,0,2,1:T(8,128)}) %all-reduce.7.cloned.1.call-update) | async-done | bytes 98320
  1089.3 0.7 constant_dynamic-slice_fusion
  1090.1 0.6 copy.40
  (108 shorter events, 7.5 us)
Async XLA Ops:
  6.5 73.7 %copy-start = (f32[256,128]{1,0:T(8,128)S(1)}, f32[256,128]{1,0:T(8,128)}, u32[]{:S(2)}) copy-start(f32[256,128]{1,0:T(8,128)} %param.10) | copy-start | bytes 393220
  6.5 898.4 %all-reduce.5.cloned.1.call-start = ((), (), s32[]{:S(2)}) async-start(), calls=%async_computation | async-start | bytes 6291456
  7.8 15.5 %collective-permute-start = (f32[16,3,1,256]{3,2,0,1:T(1,128)S(1)}, f32[16,3,1,256]{3,2,0,1:T(1,128)S(1)}, u32[]{:S(2)}, u32[]{:S(2)}) collective-permute-start(f32[16,3,1,256]{3,2,0,1:T(1,128)S(1)} %get-tuple-element.63), channel_id=1, source_target_pairs={{0,1},{1,2},{2,3},{3,4},{4,5},{5,6},{6,7},{7,8},{8,9},{9,10},{10,1... | collective-permute-start | bytes 147464 | tf_op jit(solution)/shard_map/ppermute | solution.py:21
  9.7 14.6 %collective-permute-start.1 = (f32[16,3,1,256]{3,2,0,1:T(1,128)S(1)}, f32[16,3,1,256]{3,2,0,1:T(1,128)S(1)}, u32[]{:S(2)}, u32[]{:S(2)}) collective-permute-start(f32[16,3,1,256]{3,2,0,1:T(1,128)S(1)} %get-tuple-element.64), channel_id=1, source_target_pairs={{1,0},{2,1},{3,2},{4,3},{5,4},{6,5},{7,6},{8,7},{9,8},{10,9},{11,1... | collective-permute-start | bytes 147464 | tf_op jit(solution)/shard_map/ppermute | solution.py:23
  27.0 1.0 copy-start.1
  27.1 1.0 copy-start.2
  28.2 13.4 %collective-permute-start.2 = (f32[16,3,1,256]{3,2,0,1:T(1,128)S(1)}, f32[16,3,1,256]{3,2,0,1:T(1,128)S(1)}, u32[]{:S(2)}, u32[]{:S(2)}) collective-permute-start(f32[16,3,1,256]{3,2,0,1:T(1,128)S(1)} %get-tuple-element.61), channel_id=1, source_target_pairs={{0,1},{1,2},{2,3},{3,4},{4,5},{5,6},{6,7},{7,8},{8,9},{9,10},{10,1... | collective-permute-start | bytes 147464 | tf_op jit(solution)/shard_map/ppermute | solution.py:21
  30.1 13.2 %collective-permute-start.3 = (f32[16,3,1,256]{3,2,0,1:T(1,128)S(1)}, f32[16,3,1,256]{3,2,0,1:T(1,128)S(1)}, u32[]{:S(2)}, u32[]{:S(2)}) collective-permute-start(f32[16,3,1,256]{3,2,0,1:T(1,128)S(1)} %get-tuple-element.62), channel_id=1, source_target_pairs={{1,0},{2,1},{3,2},{4,3},{5,4},{6,5},{7,6},{8,7},{9,8},{10,9},{11,1... | collective-permute-start | bytes 147464 | tf_op jit(solution)/shard_map/ppermute | solution.py:23
  45.8 13.1 %collective-permute-start.4 = (f32[16,3,1,256]{3,2,0,1:T(1,128)S(1)}, f32[16,3,1,256]{3,2,0,1:T(1,128)S(1)}, u32[]{:S(2)}, u32[]{:S(2)}) collective-permute-start(f32[16,3,1,256]{3,2,0,1:T(1,128)S(1)} %get-tuple-element.59), channel_id=1, source_target_pairs={{0,1},{1,2},{2,3},{3,4},{4,5},{5,6},{6,7},{7,8},{8,9},{9,10},{10,1... | collective-permute-start | bytes 147464 | tf_op jit(solution)/shard_map/ppermute | solution.py:21
  47.7 12.9 %collective-permute-start.5 = (f32[16,3,1,256]{3,2,0,1:T(1,128)S(1)}, f32[16,3,1,256]{3,2,0,1:T(1,128)S(1)}, u32[]{:S(2)}, u32[]{:S(2)}) collective-permute-start(f32[16,3,1,256]{3,2,0,1:T(1,128)S(1)} %get-tuple-element.60), channel_id=1, source_target_pairs={{1,0},{2,1},{3,2},{4,3},{5,4},{6,5},{7,6},{8,7},{9,8},{10,9},{11,1... | collective-permute-start | bytes 147464 | tf_op jit(solution)/shard_map/ppermute | solution.py:23
  63.0 13.3 %collective-permute-start.6 = (f32[16,3,1,256]{3,2,0,1:T(1,128)S(1)}, f32[16,3,1,256]{3,2,0,1:T(1,128)S(1)}, u32[]{:S(2)}, u32[]{:S(2)}) collective-permute-start(f32[16,3,1,256]{3,2,0,1:T(1,128)S(1)} %get-tuple-element.57), channel_id=1, source_target_pairs={{0,1},{1,2},{2,3},{3,4},{4,5},{5,6},{6,7},{7,8},{8,9},{9,10},{10,1... | collective-permute-start | bytes 147464 | tf_op jit(solution)/shard_map/ppermute | solution.py:21
  65.0 12.9 %collective-permute-start.7 = (f32[16,3,1,256]{3,2,0,1:T(1,128)S(1)}, f32[16,3,1,256]{3,2,0,1:T(1,128)S(1)}, u32[]{:S(2)}, u32[]{:S(2)}) collective-permute-start(f32[16,3,1,256]{3,2,0,1:T(1,128)S(1)} %get-tuple-element.58), channel_id=1, source_target_pairs={{1,0},{2,1},{3,2},{4,3},{5,4},{6,5},{7,6},{8,7},{9,8},{10,9},{11,1... | collective-permute-start | bytes 147464 | tf_op jit(solution)/shard_map/ppermute | solution.py:23
  80.2 0.7 copy-start.4
  88.4 816.6 %copy-start.3 = (f32[16,32]{1,0:T(8,128)S(1)}, f32[16,32]{1,0:T(8,128)}, u32[]{:S(2)}) copy-start(f32[16,32]{1,0:T(8,128)} %param.11) | copy-start | bytes 6148
  88.4 1000.9 %all-reduce.7.cloned.1.call-start = ((), (), s32[]{:S(2)}) async-start(), calls=%async_computation.1 | async-start | bytes 196608
Sparse Core Ops, SparseCore 0:
  88.5 816.3 all-reduce.4
  907.8 181.4 all-reduce.6
where the time goes:
time: 1100 us
  waiting for transfers between devices  1000 us (91%)
  starting transfers between devices  54.5 us (5%)
  between operations  15.5 us (1%)
  local copies, waits for them, and re-layouts  11.3 us (1%)
    unnamed x4, waiting for transfers between devices  995 us
    ppermute x4, starting transfers between devices, with_halo(): lax.ppermute(head, axis, [((i + 1) % count, i) for i in range(count)])  46.8 us
  transfers between devices with their start and end apart: 10, of which 6 were waited for; matrix products, arithmetic and copies ran while one was open for 0% of the time, Pallas kernels for 0%

commit v1 on v0

v1 whole, which is shorter than its diff:
```python
import functools

import jax
import jax.numpy as jnp
from jax import lax
from jax.experimental import pallas as pl
from jax.experimental.pallas import tpu as pltpu
from jax.sharding import PartitionSpec as P

Y, ZH, X, ZL, CORES = 4, 2, 4, 8, 2
STEPS = 2
DTIME = 0.2
HALO = 4
MESH = pl.DeviceIdType.MESH
HIGHEST = lax.Precision.HIGHEST


def primitive(q):
    rho, mx, my = q
    inverse = 1.0 / rho
    u = mx * inverse
    v = my * inverse
    sound = jnp.sqrt(rho)
    pressure = 0.5 * rho * rho
    cross = mx * v
    return dict(
        q=q,
        fx=(mx, mx * u + pressure, cross),
        gy=(my, cross, my * v + pressure),
        rx=jnp.abs(u) + sound,
        ry=jnp.abs(v) + sound,
    )


def faces_x(a, b):
    bound = jnp.maximum(a["rx"], b["rx"])
    return tuple(
        (fa + fb) - bound * (qb - qa)
        for fa, fb, qa, qb in zip(a["fx"], b["fx"], a["q"], b["q"])
    )


def ahead(t):
    return pltpu.roll(t, t.shape[-1] - 1, axis=t.ndim - 1)


def behind(t):
    return pltpu.roll(t, 1, axis=t.ndim - 1)


def slopes_y(a):
    bound = jnp.maximum(a["ry"], ahead(a["ry"]))
    q_next = tuple(ahead(t) for t in a["q"])
    g_next = (q_next[2], ahead(a["gy"][1]), ahead(a["gy"][2]))
    out = []
    for g, gn, q, qn in zip(a["gy"], g_next, a["q"], q_next):
        face = (g + gn) - bound * (qn - q)
        out.append(face - behind(face))
    return out


def sweep(source, store, desired_row, low, high, tile):
    def tile_step(index, carry):
        sub = pl.ds(pl.multiple_of(index * tile, tile), tile)

        def row(r):
            return primitive(tuple(source[r, c, sub, :] for c in range(3)))

        before, here = row(low - 1), row(low)
        face_before = faces_x(before, here)
        for r in range(low, high + 1):
            after = row(r + 1)
            face_after = faces_x(here, after)
            gy = slopes_y(here)
            new = []
            for c in range(3):
                flux = (face_after[c] - face_before[c]) + gy[c]
                value = here["q"][c] - (0.5 * DTIME) * flux
                if c:
                    wish = jnp.broadcast_to(desired_row(c - 1, r), value.shape)
                    value = value + DTIME * (here["q"][0] * wish - here["q"][c])
                new.append(value)
            store(r, sub, new)
            here, face_before = after, face_after
        return carry

    return tile_step


def hops(offset, extent):
    return min(offset % extent, (-offset) % extent)


def kernel(
    dens, mom, want, fx, fy, fm, out,
    strip, half, final, want_lo, want_hi, fx_all, weight, turned,
    k_out, k_in, a_out, a_in, b_out, b_in,
    h_send, h_recv, d_send, d_recv, f_send, f_recv,
    k_send, k_recv, a_send, a_recv, b_send, b_recv,
):
    members, rows, ny = dens.shape
    tile = min(members, 8)
    ry = fy.shape[1]
    kb = X
    planes = X * CORES
    nk = Y * ZH * kb
    mem, gx = lax.axis_index("mem"), lax.axis_index("gx")
    y, zh = mem // ZH, mem % ZH
    core = gx % CORES
    zl = (gx // CORES) % ZL
    x = gx // (CORES * ZL)
    xc = x * CORES + core
    z = zh * ZL + zl
    other = (zh + core) % 2

    def device(y_, zh_, x_, zl_, core_):
        return (y_ * ZH + zh_, (x_ * ZL + zl_) * CORES + core_)

    count = X * ZL * CORES
    right = (mem, (gx + 1) % count)
    left = (mem, (gx + count - 1) % count)
    near = [
        (dy, dx, dc)
        for dy in range(Y) for dx in range(X) for dc in range(CORES)
        if dy or dx or dc
    ]
    near.sort(key=lambda o: -(hops(o[0], Y) + hops(o[1], X)))

    def in_plane(dy, dx, dc):
        return (y + dy) % Y, (x + dx) % X, (core + dc) % CORES

    barrier = pltpu.get_barrier_semaphore()

    def greet(who):
        pl.semaphore_signal(barrier, inc=1, device_id=who, device_id_type=MESH)

    greet(right)
    greet(left)
    for i in range(1, ZH * ZL):
        zz = (z + i) % (ZH * ZL)
        greet(device(y, zz // ZL, x, zz % ZL, zh))

    @pl.when(other == 1)
    def _():
        greet(device(y, zh, x, zl, zh))

    for o in near:
        y_, x_, c_ = in_plane(*o)
        greet(device(y_, zh, x_, zl, c_))

    for r in range(rows):
        strip[HALO + r, 0] = dens[:, r, :]
        strip[HALO + r, 1] = mom[:, 0, r, :]
        strip[HALO + r, 2] = mom[:, 1, r, :]

    pl.semaphore_wait(barrier, 2 + (ZH * ZL - 1) + len(near) + other)

    def remote(src, dst, send, recv, who):
        return pltpu.make_async_remote_copy(
            src_ref=src, dst_ref=dst, send_sem=send, recv_sem=recv,
            device_id=who, device_id_type=MESH,
        )

    to_right = remote(
        strip.at[pl.ds(rows, HALO)], strip.at[pl.ds(0, HALO)],
        h_send.at[0], h_recv.at[0], right,
    )
    to_left = remote(
        strip.at[pl.ds(HALO, HALO)], strip.at[pl.ds(HALO + rows, HALO)],
        h_send.at[1], h_recv.at[1], left,
    )
    want_right = remote(want, want_lo, d_send.at[0], d_recv.at[0], right)
    want_left = remote(want, want_hi, d_send.at[1], d_recv.at[1], left)
    halo = [want_right, want_left, to_right, to_left]
    for copy in halo:
        copy.start()

    factor = []
    for o in near:
        if o[0] == 0:
            y_, x_, c_ = in_plane(*o)
            them = x_ * CORES + c_
            copy = remote(
                fx, fx_all.at[xc], f_send.at[them], f_recv.at[xc],
                device(y, zh, x_, zl, c_),
            )
            copy.start()
            factor.append((copy, them))
    fx_all[xc] = fx[...]

    shape = (nk * rows, rows * members)
    pick = (
        lax.broadcasted_iota(jnp.int32, (nk * rows, nk), 0) // rows
        == lax.broadcasted_iota(jnp.int32, (nk * rows, nk), 1)
    ).astype(jnp.float32)
    spread = (
        lax.broadcasted_iota(jnp.int32, (members, rows * members), 1) % members
        == lax.broadcasted_iota(jnp.int32, (members, rows * members), 0)
    ).astype(jnp.float32)
    tall = lax.dot_general(
        pick, fm[...], (((1,), (1,)), ((), ())),
        precision=HIGHEST, preferred_element_type=jnp.float32,
    )
    wide = jnp.dot(tall, spread, precision=HIGHEST, preferred_element_type=jnp.float32)
    same_row = (
        lax.broadcasted_iota(jnp.int32, shape, 0) % rows
        == lax.broadcasted_iota(jnp.int32, shape, 1) // members
    )
    weight[...] = jnp.where(same_row, wide, 0.0)

    for copy, them in factor:
        remote(fx, fx_all.at[them], f_send.at[them], f_recv.at[them], right).wait_recv()
    ranks = fx.shape[1]
    per = ranks // count
    new_a = lax.broadcasted_iota(jnp.int32, (ranks, ranks), 0)
    old_a = lax.broadcasted_iota(jnp.int32, (ranks, ranks), 1)
    t_ = new_a % per
    x_ = (new_a // per) % X
    c_ = (new_a // (per * X)) % CORES
    zl_ = new_a // (per * X * CORES)
    order = (old_a == ((x_ * ZL + zl_) * CORES + c_) * per + t_).astype(jnp.float32)
    turned[...] = lax.dot_general(
        order, fx_all[...].reshape(planes * rows, ranks), (((1,), (1,)), ((), ())),
        precision=HIGHEST, preferred_element_type=jnp.float32,
    )

    def desired_row(c, r):
        if r < HALO:
            return want_lo[c, pl.ds(rows - HALO + r, 1), :]
        if r < HALO + rows:
            return want[c, pl.ds(r - HALO, 1), :]
        return want_hi[c, pl.ds(r - HALO - rows, 1), :]

    for copy in halo:
        copy.wait_recv()
    for copy in halo:
        copy.wait_send()

    low, high = 1, rows + 2 * HALO - 2
    for step in range(STEPS):
        def keep(r, sub, new):
            for c in range(3):
                half[r, c, sub, :] = new[c]

        lax.fori_loop(
            0, members // tile, sweep(strip, keep, desired_row, low, high, tile), 0
        )
        low, high = low + 1, high - 1
        last = step == STEPS - 1

        def blend(r, sub, new):
            for c in range(3):
                value = 0.5 * strip[r, c, sub, :] + 0.5 * new[c]
                if last:
                    final[c, r - HALO, sub, :] = value
                else:
                    strip[r, c, sub, :] = value

        lax.fori_loop(
            0, members // tile, sweep(half, blend, desired_row, low, high, tile), 0
        )
        low, high = low + 1, high - 1

    along_y = jnp.dot(
        final[...].reshape(3 * rows * members, ny), fy[...],
        precision=HIGHEST, preferred_element_type=jnp.float32,
    ).reshape(3, rows * members, ry)
    for c in range(3):
        k_out[:, c] = jnp.dot(
            weight[...], along_y[c], precision=HIGHEST, preferred_element_type=jnp.float32
        ).reshape(nk, rows, ry)

    def k_of(y_, x_, c_):
        return (y_ * ZH + c_) * kb + x_

    k_copies = []
    for o in near:
        y_, x_, c_ = in_plane(*o)
        slot = y_ * planes + x_ * CORES + c_
        copy = remote(
            k_out.at[k_of(y_, x_, c_)], k_in.at[y * planes + xc],
            k_send.at[slot], k_recv.at[y * planes + xc], device(y_, zh, x_, zl, c_),
        )
        copy.start()
        k_copies.append((copy, slot))
    k_in[y * planes + xc] = k_out[k_of(y, x, core)]
    for copy, slot in reversed(k_copies):
        remote(
            k_out.at[0], k_in.at[slot], k_send.at[slot], k_recv.at[slot], right
        ).wait_recv()
    total = k_in[pl.ds(0, planes)]
    for i in range(1, Y):
        total = total + k_in[pl.ds(i * planes, planes)]

    for c in range(3):
        a_out[:, c] = jnp.dot(
            turned[...], total[:, c].reshape(planes * rows, ry),
            precision=HIGHEST, preferred_element_type=jnp.float32,
        ).reshape(ZL * CORES, per * X, ry)

    a_copies = []
    far = sorted(range(ZL), key=lambda s: (hops(s, ZL) * -1, s))
    for i in range(ZL):
        s = far[i] + other * (far[ZL - 1 - i] - far[i])
        zl_t = (zl + s) % ZL
        for d in (1, 0):
            c_t = (core + d) % CORES
            slot = zl_t * CORES + c_t
            copy = remote(
                a_out.at[slot], a_in.at[z], a_send.at[slot], a_recv.at[z],
                device(y, core, x, zl_t, c_t),
            )
            if i == ZL - 1 and d == 0:
                @pl.when(other == 1)
                def _():
                    copy.start()

                @pl.when(other == 0)
                def _():
                    a_in[z] = a_out[zl * CORES + core]
            else:
                copy.start()
                a_copies.append(copy)
            last_copy = copy

    def landed(slot):
        remote(
            a_out.at[0], a_in.at[slot], a_send.at[0], a_recv.at[slot], right
        ).wait_recv()

    @pl.when(other == 1)
    def _():
        landed(z)

    for i in range(1, ZH * ZL):
        landed((z + i) % (ZH * ZL))
    piece = a_in[0]
    for i in range(1, ZH * ZL):
        piece = piece + a_in[i]

    for i in range(X):
        b_out[i] = piece[:, i * per:(i + 1) * per, :]
    b_copies = []
    for dx in (2, 1, 3) if X == 4 else range(1, X):
        x_t = (x + dx) % X
        copy = remote(
            b_out.at[x_t], b_in.at[x], b_send.at[x_t], b_recv.at[x],
            device(y, zh, x_t, zl, core),
        )
        copy.start()
        b_copies.append((copy, x_t))
    b_in[x] = b_out[x]
    for copy, x_t in b_copies:
        remote(b_out.at[0], b_in.at[x_t], b_send.at[x_t], b_recv.at[x_t], right).wait_recv()
    out[...] = b_in[...]

    for copy, _slot in factor + k_copies + b_copies:
        copy.wait_send()
    for copy in a_copies:
        copy.wait_send()

    @pl.when(other == 1)
    def _():
        last_copy.wait_send()


def on_device(density, momenta, desired, factor_x, factor_y, factor_m):
    members, rows, ny = density.shape
    ranks = factor_x.shape[1]
    ry = factor_y.shape[1]
    count = X * ZL * CORES
    per = ranks // count
    planes = X * CORES
    nk = Y * ZH * X
    f32 = jnp.float32
    vmem = pl.BlockSpec(memory_space=pltpu.VMEM)
    dma = pltpu.SemaphoreType.DMA
    strip = (rows + 2 * HALO, 3, members, ny)
    return pl.pallas_call(
        kernel,
        out_shape=jax.ShapeDtypeStruct((X, 3, per, ry), f32),
        in_specs=[vmem] * 6,
        out_specs=vmem,
        scratch_shapes=[
            pltpu.VMEM(strip, f32),
            pltpu.VMEM(strip, f32),
            pltpu.VMEM((3, rows, members, ny), f32),
            pltpu.VMEM((2, rows, ny), f32),
            pltpu.VMEM((2, rows, ny), f32),
            pltpu.VMEM((planes, rows, ranks), f32),
            pltpu.VMEM((nk * rows, rows * members), f32),
            pltpu.VMEM((ranks, planes * rows), f32),
            pltpu.VMEM((nk, 3, rows, ry), f32),
            pltpu.VMEM((Y * planes, 3, rows, ry), f32),
            pltpu.VMEM((ZL * CORES, 3, per * X, ry), f32),
            pltpu.VMEM((ZH * ZL, 3, per * X, ry), f32),
            pltpu.VMEM((X, 3, per, ry), f32),
            pltpu.VMEM((X, 3, per, ry), f32),
            dma((2,)), dma((2,)), dma((2,)), dma((2,)),
            dma((planes,)), dma((planes,)),
            dma((Y * planes,)), dma((Y * planes,)),
            dma((ZL * CORES,)), dma((ZH * ZL,)),
            dma((X,)), dma((X,)),
        ],
        compiler_params=pltpu.CompilerParams(
            collective_id=0, has_side_effects=True, vmem_limit_bytes=48 * 1024 * 1024
        ),
    )(density, momenta, desired, factor_x, factor_y, factor_m)


def solution(mesh):
    return jax.shard_map(
        on_device,
        mesh=mesh,
        in_specs=(
            P("mem", "gx", None),
            P("mem", None, "gx", None),
            P(None, "gx", None),
            P("gx", None),
            P(),
            P("mem", None),
        ),
        out_specs=P("mem", None, "gx", None),
        check_vma=False,
    )
```

time: 1100 us -> 58 us (0.05)
  the two profiles are of different devices: /device:TPU:6 before, /device:TPU:32 now
where the time goes in v1:
time: 58 us; the launch traced here: 57.7 us
  Pallas kernels  52.2 us (90%)
  local copies, waits for them, and re-layouts  5.46 us (9%)
    pallas_call x1, Pallas kernels, on_device(): pl.pallas_call(kernel, out_shape=jax.ShapeDtypeStruct((X, 3, per, ry), f3...  52.2 us
    unnamed x13, local copies, waits for them, and re-layouts  5.46 us

profile of v1, /device:TPU:32, one launch (start us, length us, event | category | flops | bytes accessed | tf_op | source)
XLA Modules:
  0.0 57.7 jit_solution(12632334351049442756)
XLA Ops:
  0.0 0.0 copy-start
  0.0 0.9 %copy-done = f32[16,2,8,256]{3,2,1,0:T(8,128)S(1)} copy-done((f32[16,2,8,256]{3,2,1,0:T(8,128)S(1)}, f32[16,2,8,256]{3,2,1,0:T(8,128)}, u32[]{:S(2)}) %copy-start) | copy-done | bytes 262168
  1.0 0.0 copy-start.1
  1.0 0.9 %copy-done.1 = f32[16,8,256]{2,1,0:T(8,128)S(1)} copy-done((f32[16,8,256]{2,1,0:T(8,128)S(1)}, f32[16,8,256]{2,1,0:T(8,128)}, u32[]{:S(2)}) %copy-start.1) | copy-done | bytes 131096
  1.9 0.0 copy-start.2
  1.9 0.9 %copy-done.2 = f32[256,128]{1,0:T(8,128)S(1)} copy-done((f32[256,128]{1,0:T(8,128)S(1)}, f32[256,128]{1,0:T(8,128)}, u32[]{:S(2)}) %copy-start.2) | copy-done | bytes 131096
  2.8 0.0 copy-start.3
  2.8 0.7 %copy-done.3 = f32[2,8,256]{2,1,0:T(8,128)S(1)} copy-done((f32[2,8,256]{2,1,0:T(8,128)S(1)}, f32[2,8,256]{2,1,0:T(8,128)}, u32[]{:S(2)}) %copy-start.3) | copy-done | bytes 16408
  3.5 0.0 copy-start.4
  3.5 0.7 %copy-done.4 = f32[16,32]{1,0:T(8,128)S(1)} copy-done((f32[16,32]{1,0:T(8,128)S(1)}, f32[16,32]{1,0:T(8,128)}, u32[]{:S(2)}) %copy-start.4) | copy-done | bytes 2072
  4.2 0.0 copy-start.5
  4.2 0.7 %copy-done.5 = f32[8,128]{1,0:T(8,128)S(1)} copy-done((f32[8,128]{1,0:T(8,128)S(1)}, f32[8,128]{1,0:T(8,128)}, u32[]{:S(2)}) %copy-start.5) | copy-done | bytes 4120
  4.9 52.2 %shard_map.64 = f32[4,3,2,128]{3,2,1,0:T(2,128)S(1)} custom-call(f32[16,8,256]{2,1,0:T(8,128)S(1)} %copy-done.1, f32[16,2,8,256]{3,2,1,0:T(8,128)S(1)} %copy-done, f32[2,8,256]{2,1,0:T(8,128)S(1)} %copy-done.3, f32[8,128]{1,0:T(8,128)S(1)} %copy-done.5, f32[256,128]{1,0:T(8,128)S(1)} %copy-done.2, f32[16,32]{1,0:T(8,128)S(1)} %copy-done.4), custom_call_target="tpu_custom_call" | custom-call | tf_op jit(solution)/shard_map/pallas_call | solution.py:379
  57.1 0.6 %copy.8 = f32[4,3,2,128]{3,2,1,0:T(2,128)} copy(f32[4,3,2,128]{3,2,1,0:T(2,128)S(1)} %shard_map.64) | data formatting | bytes 24576
Async XLA Ops:
  0.0 0.9 %copy-start = (f32[16,2,8,256]{3,2,1,0:T(8,128)S(1)}, f32[16,2,8,256]{3,2,1,0:T(8,128)}, u32[]{:S(2)}) copy-start(f32[16,2,8,256]{3,2,1,0:T(8,128)} %mom.1) | copy-start | bytes 786436
  1.0 0.9 %copy-start.1 = (f32[16,8,256]{2,1,0:T(8,128)S(1)}, f32[16,8,256]{2,1,0:T(8,128)}, u32[]{:S(2)}) copy-start(f32[16,8,256]{2,1,0:T(8,128)} %dens.1) | copy-start | bytes 393220
  1.9 0.9 %copy-start.2 = (f32[256,128]{1,0:T(8,128)S(1)}, f32[256,128]{1,0:T(8,128)}, u32[]{:S(2)}) copy-start(f32[256,128]{1,0:T(8,128)} %fy.1) | copy-start | bytes 393220
  2.8 0.7 %copy-start.3 = (f32[2,8,256]{2,1,0:T(8,128)S(1)}, f32[2,8,256]{2,1,0:T(8,128)}, u32[]{:S(2)}) copy-start(f32[2,8,256]{2,1,0:T(8,128)} %want.1) | copy-start | bytes 49156
  3.5 0.7 %copy-start.4 = (f32[16,32]{1,0:T(8,128)S(1)}, f32[16,32]{1,0:T(8,128)}, u32[]{:S(2)}) copy-start(f32[16,32]{1,0:T(8,128)} %fm.1) | copy-start | bytes 6148
  4.2 0.7 %copy-start.5 = (f32[8,128]{1,0:T(8,128)S(1)}, f32[8,128]{1,0:T(8,128)}, u32[]{:S(2)}) copy-start(f32[8,128]{1,0:T(8,128)} %fx.1) | copy-start | bytes 12292

commit v2 on v1

--- a/solution.py
+++ b/solution.py
@@ -59,16 +59,17 @@
     return out
 
 
-def sweep(source, store, desired_row, low, high, tile):
+def sweep(source, store, desired_row, start, count, tile):
     def tile_step(index, carry):
         sub = pl.ds(pl.multiple_of(index * tile, tile), tile)
 
         def row(r):
             return primitive(tuple(source[r, c, sub, :] for c in range(3)))
 
-        before, here = row(low - 1), row(low)
+        before, here = row(start - 1), row(start)
         face_before = faces_x(before, here)
-        for r in range(low, high + 1):
+        for i in range(count):
+            r = start + i
             after = row(r + 1)
             face_after = faces_x(here, after)
             gy = slopes_y(here)
@@ -92,13 +93,14 @@
 
 
 def kernel(
-    dens, mom, want, fx, fy, fm, out,
-    strip, half, final, want_lo, want_hi, fx_all, weight, turned,
+    dens_hbm, mom_hbm, want_hbm, fx_hbm, fy_hbm, fm_hbm, out,
+    dens, mom, want, fx_all, fy, fm,
+    strip0, strip1, strip2, strip3, final, weight, turned, gathered,
     k_out, k_in, a_out, a_in, b_out, b_in,
-    h_send, h_recv, d_send, d_recv, f_send, f_recv,
+    in_sem, h_send, h_recv, d_send, d_recv, f_send, f_recv,
     k_send, k_recv, a_send, a_recv, b_send, b_recv,
 ):
-    members, rows, ny = dens.shape
+    members, rows, ny = dens_hbm.shape
     tile = min(members, 8)
     ry = fy.shape[1]
     kb = X
@@ -129,6 +131,16 @@
     def in_plane(dy, dx, dc):
         return (y + dy) % Y, (x + dx) % X, (core + dc) % CORES
 
+    fetch = [
+        pltpu.make_async_copy(src, dst, in_sem.at[i])
+        for i, (src, dst) in enumerate([
+            (dens_hbm, dens), (mom_hbm, mom), (want_hbm, want.at[:, pl.ds(rows, rows), :]),
+            (fx_hbm, fx_all.at[xc]), (fy_hbm, fy), (fm_hbm, fm),
+        ])
+    ]
+    for copy in fetch:
+        copy.start()
+
     barrier = pltpu.get_barrier_semaphore()
 
     def greet(who):
@@ -148,10 +160,12 @@
         y_, x_, c_ = in_plane(*o)
         greet(device(y_, zh, x_, zl, c_))
 
+    for copy in fetch[:2]:
+        copy.wait()
     for r in range(rows):
-        strip[HALO + r, 0] = dens[:, r, :]
-        strip[HALO + r, 1] = mom[:, 0, r, :]
-        strip[HALO + r, 2] = mom[:, 1, r, :]
+        strip0[HALO + r, 0] = dens[:, r, :]
+        strip0[HALO + r, 1] = mom[:, 0, r, :]
+        strip0[HALO + r, 2] = mom[:, 1, r, :]
 
     pl.semaphore_wait(barrier, 2 + (ZH * ZL - 1) + len(near) + other)
 
@@ -162,18 +176,32 @@
         )
 
     to_right = remote(
-        strip.at[pl.ds(rows, HALO)], strip.at[pl.ds(0, HALO)],
+        strip0.at[pl.ds(rows, HALO)], strip0.at[pl.ds(0, HALO)],
         h_send.at[0], h_recv.at[0], right,
     )
     to_left = remote(
-        strip.at[pl.ds(HALO, HALO)], strip.at[pl.ds(HALO + rows, HALO)],
+        strip0.at[pl.ds(HALO, HALO)], strip0.at[pl.ds(HALO + rows, HALO)],
         h_send.at[1], h_recv.at[1], left,
     )
-    want_right = remote(want, want_lo, d_send.at[0], d_recv.at[0], right)
-    want_left = remote(want, want_hi, d_send.at[1], d_recv.at[1], left)
-    halo = [want_right, want_left, to_right, to_left]
-    for copy in halo:
-        copy.start()
+    want_right = remote(
+        want_hbm, want.at[:, pl.ds(0, rows), :], d_send.at[0], d_recv.at[0], right
+    )
+    want_left = remote(
+        want_hbm, want.at[:, pl.ds(2 * rows, rows), :], d_send.at[1], d_recv.at[1], left
+    )
+    later_right = (core == 1) & (zl <= 2)
+    later_left = (core == 0) & (zl >= ZL - 3)
+
+    @pl.when(jnp.logical_not(later_right))
+    def _():
+        to_right.start()
+
+    @pl.when(jnp.logical_not(later_left))
+    def _():
+        to_left.start()
+
+    want_right.start()
+    want_left.start()
 
     factor = []
     for o in near:
@@ -181,21 +209,45 @@
             y_, x_, c_ = in_plane(*o)
             them = x_ * CORES + c_
             copy = remote(
-                fx, fx_all.at[xc], f_send.at[them], f_recv.at[xc],
+                fx_hbm, fx_all.at[xc], f_send.at[them], f_recv.at[xc],
                 device(y, zh, x_, zl, c_),
             )
             copy.start()
             factor.append((copy, them))
-    fx_all[xc] = fx[...]
-
-    shape = (nk * rows, rows * members)
+    for copy in fetch[2:]:
+        copy.wait()
+
+    def desired_row(c, r):
+        return want[c, pl.ds(r + rows - HALO, 1), :]
+
+    strips = (strip0, strip1, strip2, strip3)
+
+    def section(e, start, count, side=None):
+        def store(r, sub, new):
+            for c in range(3):
+                value = new[c]
+                if e % 2:
+                    value = 0.5 * strips[e - 1][r, c, sub, :] + 0.5 * value
+                if e == 2 * STEPS - 1:
+                    final[c, r - start, sub, :] = value
+                else:
+                    strips[e + 1][r, c, sub, :] = value
+
+        lax.fori_loop(
+            0, members // tile, sweep(strips[e], store, desired_row, start, count, tile), 0
+        )
+
+    for e in range(2 * STEPS - 1):
+        section(e, HALO + 1 + e, rows - 2 - 2 * e)
+
+    shape = (nk * rows, HALO * members)
     pick = (
         lax.broadcasted_iota(jnp.int32, (nk * rows, nk), 0) // rows
         == lax.broadcasted_iota(jnp.int32, (nk * rows, nk), 1)
     ).astype(jnp.float32)
     spread = (
-        lax.broadcasted_iota(jnp.int32, (members, rows * members), 1) % members
-        == lax.broadcasted_iota(jnp.int32, (members, rows * members), 0)
+        lax.broadcasted_iota(jnp.int32, (members, HALO * members), 1) % members
+        == lax.broadcasted_iota(jnp.int32, (members, HALO * members), 0)
     ).astype(jnp.float32)
     tall = lax.dot_general(
         pick, fm[...], (((1,), (1,)), ((), ())),
@@ -208,9 +260,17 @@
     )
     weight[...] = jnp.where(same_row, wide, 0.0)
 
+    @pl.when(later_right)
+    def _():
+        to_right.start()
+
+    @pl.when(later_left)
+    def _():
+        to_left.start()
+
     for copy, them in factor:
-        remote(fx, fx_all.at[them], f_send.at[them], f_recv.at[them], right).wait_recv()
-    ranks = fx.shape[1]
+        remote(fx_hbm, fx_all.at[them], f_send.at[them], f_recv.at[them], right).wait_recv()
+    ranks = fx_all.shape[2]
     per = ranks // count
     new_a = lax.broadcasted_iota(jnp.int32, (ranks, ranks), 0)
     old_a = lax.broadcasted_iota(jnp.int32, (ranks, ranks), 1)
@@ -224,77 +284,65 @@
         precision=HIGHEST, preferred_element_type=jnp.float32,
     )
 
-    def desired_row(c, r):
-        if r < HALO:
-            return want_lo[c, pl.ds(rows - HALO + r, 1), :]
-        if r < HALO + rows:
-            return want[c, pl.ds(r - HALO, 1), :]
-        return want_hi[c, pl.ds(r - HALO - rows, 1), :]
-
-    for copy in halo:
-        copy.wait_recv()
-    for copy in halo:
-        copy.wait_send()
-
-    low, high = 1, rows + 2 * HALO - 2
-    for step in range(STEPS):
-        def keep(r, sub, new):
-            for c in range(3):
-                half[r, c, sub, :] = new[c]
-
-        lax.fori_loop(
-            0, members // tile, sweep(strip, keep, desired_row, low, high, tile), 0
-        )
-        low, high = low + 1, high - 1
-        last = step == STEPS - 1
-
-        def blend(r, sub, new):
-            for c in range(3):
-                value = 0.5 * strip[r, c, sub, :] + 0.5 * new[c]
-                if last:
-                    final[c, r - HALO, sub, :] = value
-                else:
-                    strip[r, c, sub, :] = value
-
-        lax.fori_loop(
-            0, members // tile, sweep(half, blend, desired_row, low, high, tile), 0
-        )
-        low, high = low + 1, high - 1
-
-    along_y = jnp.dot(
-        final[...].reshape(3 * rows * members, ny), fy[...],
-        precision=HIGHEST, preferred_element_type=jnp.float32,
-    ).reshape(3, rows * members, ry)
-    for c in range(3):
-        k_out[:, c] = jnp.dot(
-            weight[...], along_y[c], precision=HIGHEST, preferred_element_type=jnp.float32
-        ).reshape(nk, rows, ry)
-
     def k_of(y_, x_, c_):
         return (y_ * ZH + c_) * kb + x_
 
-    k_copies = []
-    for o in near:
+    mine = y * planes + xc
+
+    def k_copy(side, o):
         y_, x_, c_ = in_plane(*o)
         slot = y_ * planes + x_ * CORES + c_
-        copy = remote(
-            k_out.at[k_of(y_, x_, c_)], k_in.at[y * planes + xc],
-            k_send.at[slot], k_recv.at[y * planes + xc], device(y_, zh, x_, zl, c_),
+        return remote(
+            k_out.at[side, k_of(y_, x_, c_)], k_in.at[side, mine],
+            k_send.at[side, slot], k_recv.at[side, mine], device(y_, zh, x_, zl, c_),
         )
-        copy.start()
-        k_copies.append((copy, slot))
-    k_in[y * planes + xc] = k_out[k_of(y, x, core)]
-    for copy, slot in reversed(k_copies):
+
+    def one_side(turn, carry):
+        side = (1 - core) + turn * (2 * core - 1)
         remote(
-            k_out.at[0], k_in.at[slot], k_send.at[slot], k_recv.at[slot], right
+            strip0.at[pl.ds(HALO, HALO)], strip0.at[pl.ds(side * (HALO + rows), HALO)],
+            h_send.at[side], h_recv.at[side], right,
         ).wait_recv()
-    total = k_in[pl.ds(0, planes)]
-    for i in range(1, Y):
-        total = total + k_in[pl.ds(i * planes, planes)]
+        remote(
+            want_hbm, want.at[:, pl.ds(pl.multiple_of(side * 2 * rows, rows), rows), :],
+            d_send.at[side], d_recv.at[side], right,
+        ).wait_recv()
+        for e in range(2 * STEPS):
+            section(e, 1 + e + side * (rows + 2 - 2 * e), HALO)
+        along_y = jnp.dot(
+            final[...].reshape(3 * HALO * members, ny), fy[...],
+            precision=HIGHEST, preferred_element_type=jnp.float32,
+        ).reshape(3, HALO * members, ry)
+        for c in range(3):
+            k_out[side, :, c] = jnp.dot(
+                weight[...], along_y[c], precision=HIGHEST, preferred_element_type=jnp.float32
+            ).reshape(nk, rows, ry)[:, :HALO]
+        for o in near:
+            k_copy(side, o).start()
+        k_in[side, mine] = k_out[side, k_of(y, x, core)]
+        return carry
+
+    lax.fori_loop(0, 2, one_side, 0)
+
+    for side in range(2):
+        for o in reversed(near):
+            y_, x_, c_ = in_plane(*o)
+            slot = y_ * planes + x_ * CORES + c_
+            remote(
+                k_out.at[0, 0], k_in.at[side, slot],
+                k_send.at[side, slot], k_recv.at[side, slot], right,
+            ).wait_recv()
+    for side in range(2):
+        total = k_in[side, pl.ds(0, planes)]
+        for i in range(1, Y):
+            total = total + k_in[side, pl.ds(i * planes, planes)]
+        for c in range(3):
+            for i in range(planes):
+                gathered[c, pl.ds(i * rows + side * HALO, HALO), :] = total[i, c]
 
     for c in range(3):
         a_out[:, c] = jnp.dot(
-            turned[...], total[:, c].reshape(planes * rows, ry),
+            turned[...], gathered[c],
             precision=HIGHEST, preferred_element_type=jnp.float32,
         ).reshape(ZL * CORES, per * X, ry)
 
@@ -354,8 +402,13 @@
         remote(b_out.at[0], b_in.at[x_t], b_send.at[x_t], b_recv.at[x_t], right).wait_recv()
     out[...] = b_in[...]
 
-    for copy, _slot in factor + k_copies + b_copies:
+    for copy, _slot in factor + b_copies:
         copy.wait_send()
+    for copy in (to_right, to_left, want_right, want_left):
+        copy.wait_send()
+    for side in range(2):
+        for o in near:
+            k_copy(side, o).wait_send()
     for copy in a_copies:
         copy.wait_send()
 
@@ -379,31 +432,37 @@
     return pl.pallas_call(
         kernel,
         out_shape=jax.ShapeDtypeStruct((X, 3, per, ry), f32),
-        in_specs=[vmem] * 6,
+        in_specs=[pl.BlockSpec(memory_space=pltpu.HBM)] * 6,
         out_specs=vmem,
         scratch_shapes=[
+            pltpu.VMEM((members, rows, ny), f32),
+            pltpu.VMEM((members, 2, rows, ny), f32),
+            pltpu.VMEM((2, 3 * rows, ny), f32),
+            pltpu.VMEM((planes, rows, ranks), f32),
+            pltpu.VMEM((ny, ry), f32),
+            pltpu.VMEM((members, factor_m.shape[1]), f32),
             pltpu.VMEM(strip, f32),
             pltpu.VMEM(strip, f32),
-            pltpu.VMEM((3, rows, members, ny), f32),
-            pltpu.VMEM((2, rows, ny), f32),
-            pltpu.VMEM((2, rows, ny), f32),
-            pltpu.VMEM((planes, rows, ranks), f32),
-            pltpu.VMEM((nk * rows, rows * members), f32),
+            pltpu.VMEM(strip, f32),
+            pltpu.VMEM(strip, f32),
+            pltpu.VMEM((3, HALO, members, ny), f32),
+            pltpu.VMEM((nk * rows, HALO * members), f32),
             pltpu.VMEM((ranks, planes * rows), f32),
-            pltpu.VMEM((nk, 3, rows, ry), f32),
-            pltpu.VMEM((Y * planes, 3, rows, ry), f32),
+            pltpu.VMEM((3, planes * rows, ry), f32),
+            pltpu.VMEM((2, nk, 3, HALO, ry), f32),
+            pltpu.VMEM((2, Y * planes, 3, HALO, ry), f32),
             pltpu.VMEM((ZL * CORES, 3, per * X, ry), f32),
             pltpu.VMEM((ZH * ZL, 3, per * X, ry), f32),
             pltpu.VMEM((X, 3, per, ry), f32),
             pltpu.VMEM((X, 3, per, ry), f32),
-            dma((2,)), dma((2,)), dma((2,)), dma((2,)),
+            dma((6,)), dma((2,)), dma((2,)), dma((2,)), dma((2,)),
             dma((planes,)), dma((planes,)),
-            dma((Y * planes,)), dma((Y * planes,)),
+            dma((2, Y * planes)), dma((2, Y * planes)),
             dma((ZL * CORES,)), dma((ZH * ZL,)),
             dma((X,)), dma((X,)),
         ],
         compiler_params=pltpu.CompilerParams(
-            collective_id=0, has_side_effects=True, vmem_limit_bytes=48 * 1024 * 1024
+            collective_id=0, has_side_effects=True, vmem_limit_bytes=67_043_328
         ),
     )(density, momenta, desired, factor_x, factor_y, factor_m)
 

time: 58 us -> 51.8 us (0.89)
  local copies, waits for them, and re-layouts: 5.46 us -> 1.31 us
  Pallas kernels: 52.2 us -> 50.3 us
    unnamed x13 -> x1, local copies, waits for them, and re-layouts: 5.46 us -> 1.31 us
    pallas_call x1, Pallas kernels: 52.2 us -> 50.3 us  [on_device(): pl.pallas_call(kernel, out_shape=jax.ShapeDtypeStruct((X, 3, per, ry), f3...]
where the time goes in v2:
time: 51.8 us; the launch traced here: 51.6 us
  Pallas kernels  50.3 us (97%)
  local copies, waits for them, and re-layouts  1.31 us (3%)
    pallas_call x1, Pallas kernels, on_device(): pl.pallas_call(kernel, out_shape=jax.ShapeDtypeStruct((X, 3, per, ry), f3...  50.3 us
    unnamed x1, local copies, waits for them, and re-layouts  1.31 us

profile of v2, /device:TPU:32, one launch (start us, length us, event | category | flops | bytes accessed | tf_op | source)
XLA Modules:
  0.0 51.6 jit_solution(18178178469172185553)
XLA Ops:
  0.0 50.3 %shard_map.64 = f32[4,3,2,128]{3,2,1,0:T(2,128)} custom-call(f32[16,8,256]{2,1,0:T(8,128)} %dens_hbm.1, f32[16,2,8,256]{3,2,1,0:T(8,128)} %mom_hbm.1, f32[2,8,256]{2,1,0:T(8,128)} %want_hbm.1, f32[8,128]{1,0:T(8,128)} %fx_hbm.1, f32[256,128]{1,0:T(8,128)} %fy_hbm.1, f32[16,32]{1,0:T(8,128)} %fm_hbm.1), custom_call_target="tpu_custom_call" | custom-call | tf_op jit(solution)/shard_map/pallas_call | solution.py:432
  50.3 1.3 %copy.8 = f32[4,3,2,128]{3,2,1,0:T(2,128)} copy(f32[4,3,2,128]{3,2,1,0:T(2,128)} %shard_map.64) | data formatting | bytes 24576

commit v3 on v2

--- a/solution.py
+++ b/solution.py
@@ -1,5 +1,3 @@
-import functools
-
 import jax
 import jax.numpy as jnp
 from jax import lax
@@ -11,6 +9,8 @@
 STEPS = 2
 DTIME = 0.2
 HALO = 4
+PAIR = 2
+TILE = 8
 MESH = pl.DeviceIdType.MESH
 HIGHEST = lax.Precision.HIGHEST
 
@@ -81,11 +81,43 @@
                     wish = jnp.broadcast_to(desired_row(c - 1, r), value.shape)
                     value = value + DTIME * (here["q"][0] * wish - here["q"][c])
                 new.append(value)
-            store(r, sub, new)
+            store(i, r, sub, new)
             here, face_before = after, face_after
         return carry
 
     return tile_step
+
+
+def halves(t):
+    top = t.astype(jnp.bfloat16)
+    return top, (t - top.astype(jnp.float32)).astype(jnp.bfloat16)
+
+
+def mul(a, b):
+    return jnp.dot(a, b, preferred_element_type=jnp.float32)
+
+
+def exact(a, b):
+    return lax.dot_general(
+        a, b, (((1,), (1,)), ((), ())),
+        precision=HIGHEST, preferred_element_type=jnp.float32,
+    )
+
+
+def index(shape, dim):
+    return lax.broadcasted_iota(jnp.int32, shape, dim)
+
+
+def one_hot(mask):
+    return mask.astype(jnp.float32)
+
+
+def interleave(low, high):
+    width = low.shape[-1]
+    first = index(low.shape, low.ndim - 1) < width // 2
+    def turn(t):
+        return pltpu.roll(t, width // 2, axis=t.ndim - 1)
+    return jnp.where(first, low, turn(high)), jnp.where(first, turn(low), high)
 
 
 def hops(offset, extent):
@@ -95,7 +127,7 @@
 def kernel(
     dens_hbm, mom_hbm, want_hbm, fx_hbm, fy_hbm, fm_hbm, out,
     dens, mom, want, fx_all, fy, fm,
-    strip0, strip1, strip2, strip3, final, weight, turned, gathered,
+    strip0, strip1, strip2, strip3, final, fy2, weight, turned,
     k_out, k_in, a_out, a_in, b_out, b_in,
     in_sem, h_send, h_recv, d_send, d_recv, f_send, f_recv,
     k_send, k_recv, a_send, a_recv, b_send, b_recv,
@@ -103,39 +135,57 @@
     members, rows, ny = dens_hbm.shape
     tile = min(members, 8)
     ry = fy.shape[1]
+    ranks = fx_all.shape[2]
     kb = X
-    planes = X * CORES
+    planes = PAIR * X * CORES
     nk = Y * ZH * kb
+    nz = ZH * ZL
+    f32 = jnp.float32
     mem, gx = lax.axis_index("mem"), lax.axis_index("gx")
-    y, zh = mem // ZH, mem % ZH
-    core = gx % CORES
-    zl = (gx // CORES) % ZL
-    x = gx // (CORES * ZL)
-    xc = x * CORES + core
+    y, zh = lax.div(mem, ZH), lax.rem(mem, ZH)
+    core = lax.rem(gx, CORES)
+    zl = lax.rem(lax.div(gx, CORES), ZL)
+    x = lax.div(gx, CORES * ZL)
+    half = lax.rem(zl, PAIR)
+    base = zl - half
     z = zh * ZL + zl
-    other = (zh + core) % 2
+    other = lax.rem(zh + core, 2)
 
     def device(y_, zh_, x_, zl_, core_):
         return (y_ * ZH + zh_, (x_ * ZL + zl_) * CORES + core_)
 
+    def source(q_, x_, c_):
+        return (q_ * X + x_) * CORES + c_
+
     count = X * ZL * CORES
-    right = (mem, (gx + 1) % count)
-    left = (mem, (gx + count - 1) % count)
+    per = ranks // count
+    right = (mem, lax.rem(gx + 1, count))
+    left = (mem, lax.rem(gx + count - 1, count))
     near = [
-        (dy, dx, dc)
-        for dy in range(Y) for dx in range(X) for dc in range(CORES)
-        if dy or dx or dc
+        (dy, dq, dx, dc)
+        for dy in range(Y) for dq in range(PAIR) for dx in range(X) for dc in range(CORES)
+        if dy or dq or dx or dc
     ]
-    near.sort(key=lambda o: -(hops(o[0], Y) + hops(o[1], X)))
-
-    def in_plane(dy, dx, dc):
-        return (y + dy) % Y, (x + dx) % X, (core + dc) % CORES
+    near.sort(key=lambda o: -(hops(o[0], Y) + o[1] + hops(o[2], X)))
+    ys = [y] + [lax.rem(y + i, Y) for i in range(1, Y)]
+    qs = [half] + [lax.rem(half + i, PAIR) for i in range(1, PAIR)]
+    xs = [x] + [lax.rem(x + i, X) for i in range(1, X)]
+    cs = [core] + [lax.rem(core + i, CORES) for i in range(1, CORES)]
+
+    def group(o):
+        return ys[o[0]], qs[o[1]], xs[o[2]], cs[o[3]]
+
+    def group_device(o):
+        y_, q_, x_, c_ = group(o)
+        return device(y_, zh, x_, base + q_, c_)
+
+    mine = y * planes + source(half, x, core)
 
     fetch = [
         pltpu.make_async_copy(src, dst, in_sem.at[i])
         for i, (src, dst) in enumerate([
             (dens_hbm, dens), (mom_hbm, mom), (want_hbm, want.at[:, pl.ds(rows, rows), :]),
-            (fx_hbm, fx_all.at[xc]), (fy_hbm, fy), (fm_hbm, fm),
+            (fx_hbm, fx_all.at[source(half, x, core)]), (fy_hbm, fy), (fm_hbm, fm),
         ])
     ]
     for copy in fetch:
@@ -148,17 +198,16 @@
 
     greet(right)
     greet(left)
-    for i in range(1, ZH * ZL):
-        zz = (z + i) % (ZH * ZL)
-        greet(device(y, zz // ZL, x, zz % ZL, zh))
+    for i in sorted(range(1, nz), key=lambda i: -hops(i, nz)):
+        zz = lax.rem(z + i, nz)
+        greet(device(y, lax.div(zz, ZL), x, lax.rem(zz, ZL), zh))
 
     @pl.when(other == 1)
     def _():
         greet(device(y, zh, x, zl, zh))
 
     for o in near:
-        y_, x_, c_ = in_plane(*o)
-        greet(device(y_, zh, x_, zl, c_))
+        greet(group_device(o))
 
     for copy in fetch[:2]:
         copy.wait()
@@ -167,7 +216,7 @@
         strip0[HALO + r, 1] = mom[:, 0, r, :]
         strip0[HALO + r, 2] = mom[:, 1, r, :]
 
-    pl.semaphore_wait(barrier, 2 + (ZH * ZL - 1) + len(near) + other)
+    pl.semaphore_wait(barrier, 2 + (nz - 1) + len(near) + other)
 
     def remote(src, dst, send, recv, who):
         return pltpu.make_async_remote_copy(
@@ -206,14 +255,13 @@
     factor = []
     for o in near:
         if o[0] == 0:
-            y_, x_, c_ = in_plane(*o)
-            them = x_ * CORES + c_
             copy = remote(
-                fx_hbm, fx_all.at[xc], f_send.at[them], f_recv.at[xc],
-                device(y, zh, x_, zl, c_),
+                fx_hbm, fx_all.at[source(half, x, core)],
+                f_send.at[source(*group(o)[1:])], f_recv.at[source(half, x, core)],
+                group_device(o),
             )
             copy.start()
-            factor.append((copy, them))
+            factor.append((copy, source(*group(o)[1:])))
     for copy in fetch[2:]:
         copy.wait()
 
@@ -222,44 +270,24 @@
 
     strips = (strip0, strip1, strip2, strip3)
 
-    def section(e, start, count, side=None):
-        def store(r, sub, new):
+    def section(e, start, n):
+        def store(i, r, sub, new):
             for c in range(3):
                 value = new[c]
                 if e % 2:
                     value = 0.5 * strips[e - 1][r, c, sub, :] + 0.5 * value
                 if e == 2 * STEPS - 1:
-                    final[c, r - start, sub, :] = value
+                    final[i // 2, c, i % 2, sub, :] = value
                 else:
                     strips[e + 1][r, c, sub, :] = value
 
         lax.fori_loop(
-            0, members // tile, sweep(strips[e], store, desired_row, start, count, tile), 0
+            0, members // tile, sweep(strips[e], store, desired_row, start, n, tile), 0
         )
 
     for e in range(2 * STEPS - 1):
         section(e, HALO + 1 + e, rows - 2 - 2 * e)
 
-    shape = (nk * rows, HALO * members)
-    pick = (
-        lax.broadcasted_iota(jnp.int32, (nk * rows, nk), 0) // rows
-        == lax.broadcasted_iota(jnp.int32, (nk * rows, nk), 1)
-    ).astype(jnp.float32)
-    spread = (
-        lax.broadcasted_iota(jnp.int32, (members, HALO * members), 1) % members
-        == lax.broadcasted_iota(jnp.int32, (members, HALO * members), 0)
-    ).astype(jnp.float32)
-    tall = lax.dot_general(
-        pick, fm[...], (((1,), (1,)), ((), ())),
-        precision=HIGHEST, preferred_element_type=jnp.float32,
-    )
-    wide = jnp.dot(tall, spread, precision=HIGHEST, preferred_element_type=jnp.float32)
-    same_row = (
-        lax.broadcasted_iota(jnp.int32, shape, 0) % rows
-        == lax.broadcasted_iota(jnp.int32, shape, 1) // members
-    )
-    weight[...] = jnp.where(same_row, wide, 0.0)
-
     @pl.when(later_right)
     def _():
         to_right.start()
@@ -267,34 +295,52 @@
     @pl.when(later_left)
     def _():
         to_left.start()
+
+    top, rest = halves(fy[...])
+    fy2[:, :ry] = top
+    fy2[:, ry:] = rest
+
+    shape = (nk * TILE, 3 * 2 * members)
+    tall = exact(one_hot(index((nk * TILE, nk), 0) // TILE == index((nk * TILE, nk), 1)), fm[...])
+    spread = one_hot(index((shape[1], members), 0) % members == index((shape[1], members), 1))
+    wide = exact(tall, spread)
+    wide = jnp.where(index(shape, 0) % TILE == index(shape, 1) // members, wide, 0.0)
+    top, rest = halves(wide)
+    weight[0] = top
+    weight[1] = rest
 
     for copy, them in factor:
         remote(fx_hbm, fx_all.at[them], f_send.at[them], f_recv.at[them], right).wait_recv()
-    ranks = fx_all.shape[2]
-    per = ranks // count
-    new_a = lax.broadcasted_iota(jnp.int32, (ranks, ranks), 0)
-    old_a = lax.broadcasted_iota(jnp.int32, (ranks, ranks), 1)
-    t_ = new_a % per
-    x_ = (new_a // per) % X
-    c_ = (new_a // (per * X)) % CORES
-    zl_ = new_a // (per * X * CORES)
-    order = (old_a == ((x_ * ZL + zl_) * CORES + c_) * per + t_).astype(jnp.float32)
-    turned[...] = lax.dot_general(
-        order, fx_all[...].reshape(planes * rows, ranks), (((1,), (1,)), ((), ())),
-        precision=HIGHEST, preferred_element_type=jnp.float32,
-    )
+    new = (per * ZL * CORES * 3 * X, ranks)
+    line = index(new, 0)
+    x_ = line % X
+    c_ = (line // (X * 3)) % CORES
+    zl_ = (line // (X * 3 * CORES)) % ZL
+    t_ = line // (X * 3 * CORES * ZL)
+    picked = exact(
+        one_hot(index(new, 1) == ((x_ * ZL + zl_) * CORES + c_) * per + t_),
+        fx_all[...].reshape(planes * rows, ranks),
+    )
+    wide = (2 * planes * TILE, planes * rows)
+    at = index(wide, 0)
+    side_, source_, row_ = at // (planes * TILE), (at // TILE) % planes, at % 2
+    both = (new[0], wide[0])
+    keep = (index(both, 0) // X) % 3 == (index(both, 1) % TILE) // 2
+    for rh in range(2):
+        place = one_hot(index(wide, 1) == source_ * rows + side_ * HALO + rh * 2 + row_)
+        top, rest = halves(jnp.where(keep, exact(picked, place), 0.0))
+        turned[rh, 0] = top
+        turned[rh, 1] = rest
 
     def k_of(y_, x_, c_):
         return (y_ * ZH + c_) * kb + x_
 
-    mine = y * planes + xc
-
     def k_copy(side, o):
-        y_, x_, c_ = in_plane(*o)
-        slot = y_ * planes + x_ * CORES + c_
+        y_, q_, x_, c_ = group(o)
+        slot = y_ * planes + source(q_, x_, c_)
         return remote(
-            k_out.at[side, k_of(y_, x_, c_)], k_in.at[side, mine],
-            k_send.at[side, slot], k_recv.at[side, mine], device(y_, zh, x_, zl, c_),
+            k_out.at[side, k_of(y_, x_, c_), q_], k_in.at[side, mine],
+            k_send.at[side, slot], k_recv.at[side, mine], group_device(o),
         )
 
     def one_side(turn, carry):
@@ -309,50 +355,56 @@
         ).wait_recv()
         for e in range(2 * STEPS):
             section(e, 1 + e + side * (rows + 2 - 2 * e), HALO)
-        along_y = jnp.dot(
-            final[...].reshape(3 * HALO * members, ny), fy[...],
-            precision=HIGHEST, preferred_element_type=jnp.float32,
-        ).reshape(3, HALO * members, ry)
-        for c in range(3):
-            k_out[side, :, c] = jnp.dot(
-                weight[...], along_y[c], precision=HIGHEST, preferred_element_type=jnp.float32
-            ).reshape(nk, rows, ry)[:, :HALO]
+        top, rest = halves(final[...].reshape(2 * 3 * 2 * members, ny))
+        twice = mul(top, fy2[...])
+        along_y = twice[:, :ry] + twice[:, ry:] + mul(rest, fy2[:, :ry])
+        deep = 3 * 2 * members
+        top, rest = halves(jnp.concatenate([along_y[:deep], along_y[deep:]], axis=1))
+        terms = mul(weight[0], top) + mul(weight[0], rest) + mul(weight[1], top)
+        parts = interleave(terms[:, :ry], terms[:, ry:])
+        for q_ in range(PAIR):
+            k_out[side, :, q_] = parts[q_].reshape(nk, TILE, ry)
         for o in near:
             k_copy(side, o).start()
-        k_in[side, mine] = k_out[side, k_of(y, x, core)]
+        k_in[side, mine] = k_out[side, k_of(y, x, core), half]
         return carry
 
     lax.fori_loop(0, 2, one_side, 0)
 
     for side in range(2):
         for o in reversed(near):
-            y_, x_, c_ = in_plane(*o)
-            slot = y_ * planes + x_ * CORES + c_
+            y_, q_, x_, c_ = group(o)
+            slot = y_ * planes + source(q_, x_, c_)
             remote(
-                k_out.at[0, 0], k_in.at[side, slot],
+                k_out.at[0, 0, 0], k_in.at[side, slot],
                 k_send.at[side, slot], k_recv.at[side, slot], right,
             ).wait_recv()
-    for side in range(2):
-        total = k_in[side, pl.ds(0, planes)]
-        for i in range(1, Y):
-            total = total + k_in[side, pl.ds(i * planes, planes)]
-        for c in range(3):
-            for i in range(planes):
-                gathered[c, pl.ds(i * rows + side * HALO, HALO), :] = total[i, c]
-
-    for c in range(3):
-        a_out[:, c] = jnp.dot(
-            turned[...], gathered[c],
-            precision=HIGHEST, preferred_element_type=jnp.float32,
-        ).reshape(ZL * CORES, per * X, ry)
+    total = k_in[:, pl.ds(0, planes)]
+    for i in range(1, Y):
+        total = total + k_in[:, pl.ds(i * planes, planes)]
+
+    top, rest = halves(total.reshape(2 * planes * TILE, ry))
+    cat = jnp.concatenate([top, rest], axis=1)
+
+    def expand(rh):
+        twice = mul(turned[rh, 0], cat)
+        return twice[:, :ry] + twice[:, ry:] + mul(turned[rh, 1], top)
+
+    even = expand(0)
+    odd = expand(1)
+    summed = even + pltpu.roll(odd, ry // 2, axis=1)
+    mid = new[0] // per
+    packed = interleave(summed[:mid], summed[mid:])[0]
+    for i in range(ZL * CORES * 3):
+        a_out[i // 3, i % 3] = packed[i * X:(i + 1) * X]
 
     a_copies = []
     far = sorted(range(ZL), key=lambda s: (hops(s, ZL) * -1, s))
     for i in range(ZL):
         s = far[i] + other * (far[ZL - 1 - i] - far[i])
-        zl_t = (zl + s) % ZL
+        zl_t = lax.rem(zl + s, ZL)
         for d in (1, 0):
-            c_t = (core + d) % CORES
+            c_t = cs[d]
             slot = zl_t * CORES + c_t
             copy = remote(
                 a_out.at[slot], a_in.at[z], a_send.at[slot], a_recv.at[z],
@@ -380,23 +432,27 @@
     def _():
         landed(z)
 
-    for i in range(1, ZH * ZL):
-        landed((z + i) % (ZH * ZL))
-    piece = a_in[0]
-    for i in range(1, ZH * ZL):
-        piece = piece + a_in[i]
+    for i in range(1, nz):
+        landed(lax.rem(z + i, nz))
+    pieces = []
+    for q_ in range(PAIR):
+        piece = a_in[q_]
+        for i in range(PAIR, nz, PAIR):
+            piece = piece + a_in[i + q_]
+        pieces.append(piece)
+    pieces = interleave(*pieces)
 
     for i in range(X):
-        b_out[i] = piece[:, i * per:(i + 1) * per, :]
+        for t in range(per):
+            b_out[i, :, t] = pieces[t][:, i]
     b_copies = []
-    for dx in (2, 1, 3) if X == 4 else range(1, X):
-        x_t = (x + dx) % X
+    for dx in (2, 1, 3):
         copy = remote(
-            b_out.at[x_t], b_in.at[x], b_send.at[x_t], b_recv.at[x],
-            device(y, zh, x_t, zl, core),
+            b_out.at[xs[dx]], b_in.at[x], b_send.at[xs[dx]], b_recv.at[x],
+            device(y, zh, xs[dx], zl, core),
         )
         copy.start()
-        b_copies.append((copy, x_t))
+        b_copies.append((copy, xs[dx]))
     b_in[x] = b_out[x]
     for copy, x_t in b_copies:
         remote(b_out.at[0], b_in.at[x_t], b_send.at[x_t], b_recv.at[x_t], right).wait_recv()
@@ -423,7 +479,7 @@
     ry = factor_y.shape[1]
     count = X * ZL * CORES
     per = ranks // count
-    planes = X * CORES
+    planes = PAIR * X * CORES
     nk = Y * ZH * X
     f32 = jnp.float32
     vmem = pl.BlockSpec(memory_space=pltpu.VMEM)
@@ -445,14 +501,14 @@
             pltpu.VMEM(strip, f32),
             pltpu.VMEM(strip, f32),
             pltpu.VMEM(strip, f32),
-            pltpu.VMEM((3, HALO, members, ny), f32),
-            pltpu.VMEM((nk * rows, HALO * members), f32),
-            pltpu.VMEM((ranks, planes * rows), f32),
-            pltpu.VMEM((3, planes * rows, ry), f32),
-            pltpu.VMEM((2, nk, 3, HALO, ry), f32),
-            pltpu.VMEM((2, Y * planes, 3, HALO, ry), f32),
-            pltpu.VMEM((ZL * CORES, 3, per * X, ry), f32),
-            pltpu.VMEM((ZH * ZL, 3, per * X, ry), f32),
+            pltpu.VMEM((2, 3, 2, members, ny), f32),
+            pltpu.VMEM((ny, 2 * ry), jnp.bfloat16),
+            pltpu.VMEM((2, nk * TILE, 3 * 2 * members), jnp.bfloat16),
+            pltpu.VMEM((2, 2, per * ZL * CORES * 3 * X, 2 * planes * TILE), jnp.bfloat16),
+            pltpu.VMEM((2, nk, PAIR, TILE, ry), f32),
+            pltpu.VMEM((2, Y * planes, TILE, ry), f32),
+            pltpu.VMEM((ZL * CORES, 3, X, ry), f32),
+            pltpu.VMEM((ZH * ZL, 3, X, ry), f32),
             pltpu.VMEM((X, 3, per, ry), f32),
             pltpu.VMEM((X, 3, per, ry), f32),
             dma((6,)), dma((2,)), dma((2,)), dma((2,)), dma((2,)),

time: 51.8 us -> 54.1 us (1.044)
  Pallas kernels: 50.3 us -> 52.6 us
    pallas_call x1, Pallas kernels: 50.3 us -> 52.6 us  [on_device(): pl.pallas_call(kernel, out_shape=jax.ShapeDtypeStruct((X, 3, per, ry), f3...]
where the time goes in v3:
time: 54.1 us; the launch traced here: 53.9 us
  Pallas kernels  52.6 us (97%)
  local copies, waits for them, and re-layouts  1.31 us (2%)
    pallas_call x1, Pallas kernels, on_device(): pl.pallas_call(kernel, out_shape=jax.ShapeDtypeStruct((X, 3, per, ry), f3...  52.6 us
    unnamed x1, local copies, waits for them, and re-layouts  1.31 us

profile of v3, /device:TPU:32, one launch (start us, length us, event | category | flops | bytes accessed | tf_op | source)
XLA Modules:
  0.0 53.9 jit_solution(7916260249549820696)
XLA Ops:
  0.0 52.6 %shard_map.64 = f32[4,3,2,128]{3,2,1,0:T(2,128)} custom-call(f32[16,8,256]{2,1,0:T(8,128)} %dens_hbm.1, f32[16,2,8,256]{3,2,1,0:T(8,128)} %mom_hbm.1, f32[2,8,256]{2,1,0:T(8,128)} %want_hbm.1, f32[8,128]{1,0:T(8,128)} %fx_hbm.1, f32[256,128]{1,0:T(8,128)} %fy_hbm.1, f32[16,32]{1,0:T(8,128)} %fm_hbm.1), custom_call_target="tpu_custom_call" | custom-call | tf_op jit(solution)/shard_map/pallas_call | solution.py:488
  52.6 1.3 %copy.8 = f32[4,3,2,128]{3,2,1,0:T(2,128)} copy(f32[4,3,2,128]{3,2,1,0:T(2,128)} %shard_map.64) | data formatting | bytes 24576

commit v4 on v2

--- a/solution.py
+++ b/solution.py
@@ -1,5 +1,3 @@
-import functools
-
 import jax
 import jax.numpy as jnp
 from jax import lax
@@ -17,10 +15,11 @@
 
 def primitive(q):
     rho, mx, my = q
-    inverse = 1.0 / rho
+    root = lax.rsqrt(rho)
+    inverse = root * root
     u = mx * inverse
     v = my * inverse
-    sound = jnp.sqrt(rho)
+    sound = rho * root
     pressure = 0.5 * rho * rho
     cross = mx * v
     return dict(
@@ -88,6 +87,15 @@
     return tile_step
 
 
+def halves(t):
+    top = t.astype(jnp.bfloat16)
+    return top, (t - top.astype(jnp.float32)).astype(jnp.bfloat16)
+
+
+def mul(a, b):
+    return jnp.dot(a, b, preferred_element_type=jnp.float32)
+
+
 def hops(offset, extent):
     return min(offset % extent, (-offset) % extent)
 
@@ -95,9 +103,9 @@
 def kernel(
     dens_hbm, mom_hbm, want_hbm, fx_hbm, fy_hbm, fm_hbm, out,
     dens, mom, want, fx_all, fy, fm,
-    strip0, strip1, strip2, strip3, final, weight, turned, gathered,
+    strip0, strip1, strip2, strip3, final, fy2, weight, turned, gathered,
     k_out, k_in, a_out, a_in, b_out, b_in,
-    in_sem, h_send, h_recv, d_send, d_recv, f_send, f_recv,
+    rounds, in_sem, h_send, h_recv, d_send, d_recv, f_send, f_recv,
     k_send, k_recv, a_send, a_recv, b_send, b_recv,
 ):
     members, rows, ny = dens_hbm.shape
@@ -107,20 +115,21 @@
     planes = X * CORES
     nk = Y * ZH * kb
     mem, gx = lax.axis_index("mem"), lax.axis_index("gx")
-    y, zh = mem // ZH, mem % ZH
-    core = gx % CORES
-    zl = (gx // CORES) % ZL
-    x = gx // (CORES * ZL)
+    y, zh = lax.div(mem, ZH), lax.rem(mem, ZH)
+    core = lax.rem(gx, CORES)
+    zl = lax.rem(lax.div(gx, CORES), ZL)
+    x = lax.div(gx, CORES * ZL)
     xc = x * CORES + core
     z = zh * ZL + zl
-    other = (zh + core) % 2
+    nz = ZH * ZL
+    other = lax.rem(zh + core, 2)
 
     def device(y_, zh_, x_, zl_, core_):
         return (y_ * ZH + zh_, (x_ * ZL + zl_) * CORES + core_)
 
     count = X * ZL * CORES
-    right = (mem, (gx + 1) % count)
-    left = (mem, (gx + count - 1) % count)
+    right = (mem, lax.rem(gx + 1, count))
+    left = (mem, lax.rem(gx + count - 1, count))
     near = [
         (dy, dx, dc)
         for dy in range(Y) for dx in range(X) for dc in range(CORES)
@@ -128,8 +137,12 @@
     ]
     near.sort(key=lambda o: -(hops(o[0], Y) + hops(o[1], X)))
 
+    ys = [y] + [lax.rem(y + i, Y) for i in range(1, Y)]
+    xs = [x] + [lax.rem(x + i, X) for i in range(1, X)]
+    cs = [core] + [lax.rem(core + i, CORES) for i in range(1, CORES)]
+
     def in_plane(dy, dx, dc):
-        return (y + dy) % Y, (x + dx) % X, (core + dc) % CORES
+        return ys[dy], xs[dx], cs[dc]
 
     fetch = [
         pltpu.make_async_copy(src, dst, in_sem.at[i])
@@ -143,22 +156,19 @@
 
     barrier = pltpu.get_barrier_semaphore()
 
-    def greet(who):
-        pl.semaphore_signal(barrier, inc=1, device_id=who, device_id_type=MESH)
-
-    greet(right)
-    greet(left)
-    for i in range(1, ZH * ZL):
-        zz = (z + i) % (ZH * ZL)
-        greet(device(y, zz // ZL, x, zz % ZL, zh))
-
-    @pl.when(other == 1)
-    def _():
-        greet(device(y, zh, x, zl, zh))
-
-    for o in near:
-        y_, x_, c_ = in_plane(*o)
-        greet(device(y_, zh, x_, zl, c_))
+    def tell(semaphore, who):
+        pl.semaphore_signal(semaphore, inc=1, device_id=who, device_id_type=MESH)
+
+    def along_z(i):
+        zz = lax.rem(z + i, nz)
+        return device(y, lax.div(zz, ZL), x, lax.rem(zz, ZL), core)
+
+    mate = device(y, zh, x, zl, cs[1])
+    y_peers = [device(ys[i], zh, x, zl, core) for i in range(1, Y)]
+    x_peers = [device(y, zh, xs[i], zl, core) for i in range(1, X)]
+    greeted = [right, left] + y_peers + x_peers + [along_z(1), along_z(nz - 1)]
+    for who in greeted:
+        tell(barrier, who)
 
     for copy in fetch[:2]:
         copy.wait()
@@ -167,7 +177,7 @@
         strip0[HALO + r, 1] = mom[:, 0, r, :]
         strip0[HALO + r, 2] = mom[:, 1, r, :]
 
-    pl.semaphore_wait(barrier, 2 + (ZH * ZL - 1) + len(near) + other)
+    pl.semaphore_wait(barrier, len(greeted))
 
     def remote(src, dst, send, recv, who):
         return pltpu.make_async_remote_copy(
@@ -202,18 +212,10 @@
 
     want_right.start()
     want_left.start()
-
-    factor = []
-    for o in near:
-        if o[0] == 0:
-            y_, x_, c_ = in_plane(*o)
-            them = x_ * CORES + c_
-            copy = remote(
-                fx_hbm, fx_all.at[xc], f_send.at[them], f_recv.at[xc],
-                device(y, zh, x_, zl, c_),
-            )
-            copy.start()
-            factor.append((copy, them))
+    second = x_peers + [along_z(1), along_z(nz - 1)]
+    for who in second:
+        tell(rounds.at[0], who)
+
     for copy in fetch[2:]:
         copy.wait()
 
@@ -239,6 +241,19 @@
 
     for e in range(2 * STEPS - 1):
         section(e, HALO + 1 + e, rows - 2 - 2 * e)
+
+    pl.semaphore_wait(rounds.at[0], len(second))
+    third = [mate, along_z(2), along_z(nz - 2)]
+    for who in third:
+        tell(rounds.at[1], who)
+
+    @pl.when(later_right)
+    def _():
+        to_right.start()
+
+    @pl.when(later_left)
+    def _():
+        to_left.start()
 
     shape = (nk * rows, HALO * members)
     pick = (
@@ -258,16 +273,29 @@
         lax.broadcasted_iota(jnp.int32, shape, 0) % rows
         == lax.broadcasted_iota(jnp.int32, shape, 1) // members
     )
-    weight[...] = jnp.where(same_row, wide, 0.0)
-
-    @pl.when(later_right)
-    def _():
-        to_right.start()
-
-    @pl.when(later_left)
-    def _():
-        to_left.start()
-
+    top, rest = halves(jnp.where(same_row, wide, 0.0))
+    weight[0] = top
+    weight[1] = rest
+    top, rest = halves(fy[...])
+    fy2[:, :ry] = top
+    fy2[:, ry:] = rest
+
+    pl.semaphore_wait(rounds.at[1], len(third))
+    fourth = [along_z(4), along_z(nz - 4)]
+    for who in fourth:
+        tell(rounds.at[2], who)
+
+    factor = []
+    for o in near:
+        if o[0] == 0:
+            y_, x_, c_ = in_plane(*o)
+            them = x_ * CORES + c_
+            copy = remote(
+                fx_hbm, fx_all.at[xc], f_send.at[them], f_recv.at[xc],
+                device(y, zh, x_, zl, c_),
+            )
+            copy.start()
+            factor.append((copy, them))
     for copy, them in factor:
         remote(fx_hbm, fx_all.at[them], f_send.at[them], f_recv.at[them], right).wait_recv()
     ranks = fx_all.shape[2]
@@ -279,10 +307,12 @@
     c_ = (new_a // (per * X)) % CORES
     zl_ = new_a // (per * X * CORES)
     order = (old_a == ((x_ * ZL + zl_) * CORES + c_) * per + t_).astype(jnp.float32)
-    turned[...] = lax.dot_general(
+    top, rest = halves(lax.dot_general(
         order, fx_all[...].reshape(planes * rows, ranks), (((1,), (1,)), ((), ())),
         precision=HIGHEST, preferred_element_type=jnp.float32,
-    )
+    ))
+    turned[0] = top
+    turned[1] = rest
 
     def k_of(y_, x_, c_):
         return (y_ * ZH + c_) * kb + x_
@@ -309,20 +339,23 @@
         ).wait_recv()
         for e in range(2 * STEPS):
             section(e, 1 + e + side * (rows + 2 - 2 * e), HALO)
-        along_y = jnp.dot(
-            final[...].reshape(3 * HALO * members, ny), fy[...],
-            precision=HIGHEST, preferred_element_type=jnp.float32,
-        ).reshape(3, HALO * members, ry)
+        top, rest = halves(final[...].reshape(3 * HALO * members, ny))
+        twice = mul(top, fy2[...])
+        along_y = twice[:, :ry] + twice[:, ry:] + mul(rest, fy2[:, :ry])
+        top, rest = halves(along_y.reshape(3, HALO * members, ry))
         for c in range(3):
-            k_out[side, :, c] = jnp.dot(
-                weight[...], along_y[c], precision=HIGHEST, preferred_element_type=jnp.float32
-            ).reshape(nk, rows, ry)[:, :HALO]
+            twice = mul(weight[0], jnp.concatenate([top[c], rest[c]], axis=1))
+            terms = twice[:, :ry] + twice[:, ry:] + mul(weight[1], top[c])
+            k_out[side, :, c] = terms.reshape(nk, rows, ry)[:, :HALO]
         for o in near:
             k_copy(side, o).start()
         k_in[side, mine] = k_out[side, k_of(y, x, core)]
         return carry
 
     lax.fori_loop(0, 2, one_side, 0)
+
+    pl.semaphore_wait(rounds.at[2], len(fourth))
+    tell(rounds.at[3], mate)
 
     for side in range(2):
         for o in reversed(near):
@@ -341,18 +374,20 @@
                 gathered[c, pl.ds(i * rows + side * HALO, HALO), :] = total[i, c]
 
     for c in range(3):
-        a_out[:, c] = jnp.dot(
-            turned[...], gathered[c],
-            precision=HIGHEST, preferred_element_type=jnp.float32,
+        top, rest = halves(gathered[c])
+        twice = mul(turned[0], jnp.concatenate([top, rest], axis=1))
+        a_out[:, c] = (
+            twice[:, :ry] + twice[:, ry:] + mul(turned[1], top)
         ).reshape(ZL * CORES, per * X, ry)
 
+    pl.semaphore_wait(rounds.at[3], 1)
     a_copies = []
     far = sorted(range(ZL), key=lambda s: (hops(s, ZL) * -1, s))
     for i in range(ZL):
         s = far[i] + other * (far[ZL - 1 - i] - far[i])
-        zl_t = (zl + s) % ZL
+        zl_t = lax.rem(zl + s, ZL)
         for d in (1, 0):
-            c_t = (core + d) % CORES
+            c_t = cs[d]
             slot = zl_t * CORES + c_t
             copy = remote(
                 a_out.at[slot], a_in.at[z], a_send.at[slot], a_recv.at[z],
@@ -381,7 +416,7 @@
         landed(z)
 
     for i in range(1, ZH * ZL):
-        landed((z + i) % (ZH * ZL))
+        landed(lax.rem(z + i, nz))
     piece = a_in[0]
     for i in range(1, ZH * ZL):
         piece = piece + a_in[i]
@@ -390,7 +425,7 @@
         b_out[i] = piece[:, i * per:(i + 1) * per, :]
     b_copies = []
     for dx in (2, 1, 3) if X == 4 else range(1, X):
-        x_t = (x + dx) % X
+        x_t = xs[dx]
         copy = remote(
             b_out.at[x_t], b_in.at[x], b_send.at[x_t], b_recv.at[x],
             device(y, zh, x_t, zl, core),
@@ -446,8 +481,9 @@
             pltpu.VMEM(strip, f32),
             pltpu.VMEM(strip, f32),
             pltpu.VMEM((3, HALO, members, ny), f32),
-            pltpu.VMEM((nk * rows, HALO * members), f32),
-            pltpu.VMEM((ranks, planes * rows), f32),
+            pltpu.VMEM((ny, 2 * ry), jnp.bfloat16),
+            pltpu.VMEM((2, nk * rows, HALO * members), jnp.bfloat16),
+            pltpu.VMEM((2, ranks, planes * rows), jnp.bfloat16),
             pltpu.VMEM((3, planes * rows, ry), f32),
             pltpu.VMEM((2, nk, 3, HALO, ry), f32),
             pltpu.VMEM((2, Y * planes, 3, HALO, ry), f32),
@@ -455,7 +491,7 @@
             pltpu.VMEM((ZH * ZL, 3, per * X, ry), f32),
             pltpu.VMEM((X, 3, per, ry), f32),
             pltpu.VMEM((X, 3, per, ry), f32),
-            dma((6,)), dma((2,)), dma((2,)), dma((2,)), dma((2,)),
+            pltpu.SemaphoreType.REGULAR((4,)), dma((6,)), dma((2,)), dma((2,)), dma((2,)), dma((2,)),
             dma((planes,)), dma((planes,)),
             dma((2, Y * planes)), dma((2, Y * planes)),
             dma((ZL * CORES,)), dma((ZH * ZL,)),

time: 51.8 us -> 52.8 us (1.019)
  the two profiles are of different devices: /device:TPU:32 before, /device:TPU:64 now
where the time goes in v4:
time: 52.8 us; the launch traced here: 52.6 us
  Pallas kernels  51.3 us (97%)
  local copies, waits for them, and re-layouts  1.31 us (2%)
    pallas_call x1, Pallas kernels, on_device(): pl.pallas_call(kernel, out_shape=jax.ShapeDtypeStruct((X, 3, per, ry), f3...  51.3 us
    unnamed x1, local copies, waits for them, and re-layouts  1.31 us

profile of v4, /device:TPU:64, one launch (start us, length us, event | category | flops | bytes accessed | tf_op | source)
XLA Modules:
  0.0 52.6 jit_solution(4833067508364230015)
XLA Ops:
  0.0 51.3 %shard_map.64 = f32[4,3,2,128]{3,2,1,0:T(2,128)} custom-call(f32[16,8,256]{2,1,0:T(8,128)} %dens_hbm.1, f32[16,2,8,256]{3,2,1,0:T(8,128)} %mom_hbm.1, f32[2,8,256]{2,1,0:T(8,128)} %want_hbm.1, f32[8,128]{1,0:T(8,128)} %fx_hbm.1, f32[256,128]{1,0:T(8,128)} %fy_hbm.1, f32[16,32]{1,0:T(8,128)} %fm_hbm.1), custom_call_target="tpu_custom_call" | custom-call | tf_op jit(solution)/shard_map/pallas_call | solution.py:467
  51.3 1.3 %copy.8 = f32[4,3,2,128]{3,2,1,0:T(2,128)} copy(f32[4,3,2,128]{3,2,1,0:T(2,128)} %shard_map.64) | data formatting | bytes 24576

commit v5 on v4

--- a/solution.py
+++ b/solution.py
@@ -242,11 +242,6 @@
     for e in range(2 * STEPS - 1):
         section(e, HALO + 1 + e, rows - 2 - 2 * e)
 
-    pl.semaphore_wait(rounds.at[0], len(second))
-    third = [mate, along_z(2), along_z(nz - 2)]
-    for who in third:
-        tell(rounds.at[1], who)
-
     @pl.when(later_right)
     def _():
         to_right.start()
@@ -280,39 +275,22 @@
     fy2[:, :ry] = top
     fy2[:, ry:] = rest
 
-    pl.semaphore_wait(rounds.at[1], len(third))
+    pl.semaphore_wait(rounds.at[0], len(second))
+    third = [mate, along_z(2), along_z(nz - 2)]
+    for who in third:
+        tell(rounds.at[1], who)
+
+    factor = [
+        (
+            remote(
+                fx_hbm, fx_all.at[xc], f_send.at[xs[dx] * CORES + cs[dc]], f_recv.at[xc],
+                device(y, zh, xs[dx], zl, cs[dc]),
+            ),
+            xs[dx] * CORES + cs[dc],
+        )
+        for dy, dx, dc in near if dy == 0
+    ]
     fourth = [along_z(4), along_z(nz - 4)]
-    for who in fourth:
-        tell(rounds.at[2], who)
-
-    factor = []
-    for o in near:
-        if o[0] == 0:
-            y_, x_, c_ = in_plane(*o)
-            them = x_ * CORES + c_
-            copy = remote(
-                fx_hbm, fx_all.at[xc], f_send.at[them], f_recv.at[xc],
-                device(y, zh, x_, zl, c_),
-            )
-            copy.start()
-            factor.append((copy, them))
-    for copy, them in factor:
-        remote(fx_hbm, fx_all.at[them], f_send.at[them], f_recv.at[them], right).wait_recv()
-    ranks = fx_all.shape[2]
-    per = ranks // count
-    new_a = lax.broadcasted_iota(jnp.int32, (ranks, ranks), 0)
-    old_a = lax.broadcasted_iota(jnp.int32, (ranks, ranks), 1)
-    t_ = new_a % per
-    x_ = (new_a // per) % X
-    c_ = (new_a // (per * X)) % CORES
-    zl_ = new_a // (per * X * CORES)
-    order = (old_a == ((x_ * ZL + zl_) * CORES + c_) * per + t_).astype(jnp.float32)
-    top, rest = halves(lax.dot_general(
-        order, fx_all[...].reshape(planes * rows, ranks), (((1,), (1,)), ((), ())),
-        precision=HIGHEST, preferred_element_type=jnp.float32,
-    ))
-    turned[0] = top
-    turned[1] = rest
 
     def k_of(y_, x_, c_):
         return (y_ * ZH + c_) * kb + x_
@@ -347,8 +325,21 @@
             twice = mul(weight[0], jnp.concatenate([top[c], rest[c]], axis=1))
             terms = twice[:, :ry] + twice[:, ry:] + mul(weight[1], top[c])
             k_out[side, :, c] = terms.reshape(nk, rows, ry)[:, :HALO]
+
+        @pl.when(turn == 0)
+        def _():
+            pl.semaphore_wait(rounds.at[1], len(third))
+            for who in fourth:
+                tell(rounds.at[2], who)
+
         for o in near:
             k_copy(side, o).start()
+
+        @pl.when(turn == 0)
+        def _():
+            for copy, _slot in factor:
+                copy.start()
+
         k_in[side, mine] = k_out[side, k_of(y, x, core)]
         return carry
 
@@ -356,6 +347,25 @@
 
     pl.semaphore_wait(rounds.at[2], len(fourth))
     tell(rounds.at[3], mate)
+
+    for copy, them in factor:
+        remote(fx_hbm, fx_all.at[them], f_send.at[them], f_recv.at[them], right).wait_recv()
+    ranks = fx_all.shape[2]
+    per = ranks // count
+    new_a = lax.broadcasted_iota(jnp.int32, (ranks, ranks), 0)
+    old_a = lax.broadcasted_iota(jnp.int32, (ranks, ranks), 1)
+    t_ = new_a % per
+    x_ = (new_a // per) % X
+    c_ = (new_a // (per * X)) % CORES
+    zl_ = new_a // (per * X * CORES)
+    order = (old_a == ((x_ * ZL + zl_) * CORES + c_) * per + t_).astype(jnp.float32)
+    top, rest = halves(lax.dot_general(
+        order, fx_all[...].reshape(planes * rows, ranks), (((1,), (1,)), ((), ())),
+        precision=HIGHEST, preferred_element_type=jnp.float32,
+    ))
+    turned[0] = top
+    turned[1] = rest
+
 
     for side in range(2):
         for o in reversed(near):

time: 52.8 us -> 48.4 us (0.917)
  the two profiles are of different devices: /device:TPU:64 before, /device:TPU:32 now
where the time goes in v5:
time: 48.4 us; the launch traced here: 48.2 us
  Pallas kernels  46.9 us (97%)
  local copies, waits for them, and re-layouts  1.31 us (3%)
    pallas_call x1, Pallas kernels, on_device(): pl.pallas_call(kernel, out_shape=jax.ShapeDtypeStruct((X, 3, per, ry), f3...  46.9 us
    unnamed x1, local copies, waits for them, and re-layouts  1.31 us

profile of v5, /device:TPU:32, one launch (start us, length us, event | category | flops | bytes accessed | tf_op | source)
XLA Modules:
  0.0 48.2 jit_solution(5327049766660435874)
XLA Ops:
  0.0 46.9 %shard_map.64 = f32[4,3,2,128]{3,2,1,0:T(2,128)} custom-call(f32[16,8,256]{2,1,0:T(8,128)} %dens_hbm.1, f32[16,2,8,256]{3,2,1,0:T(8,128)} %mom_hbm.1, f32[2,8,256]{2,1,0:T(8,128)} %want_hbm.1, f32[8,128]{1,0:T(8,128)} %fx_hbm.1, f32[256,128]{1,0:T(8,128)} %fy_hbm.1, f32[16,32]{1,0:T(8,128)} %fm_hbm.1), custom_call_target="tpu_custom_call" | custom-call | tf_op jit(solution)/shard_map/pallas_call | solution.py:477
  46.9 1.3 %copy.8 = f32[4,3,2,128]{3,2,1,0:T(2,128)} copy(f32[4,3,2,128]{3,2,1,0:T(2,128)} %shard_map.64) | data formatting | bytes 24576
